TPU v7x, 32 devices: a whole 2x2x4 slice. The times are simulated.
32 devices in a mesh: depth: 8 (over y, x, core), row: 4 (over z).
Axes of the slice: x: 2, y: 2, z: 4, core: 2. Of those that a mesh axis runs over, the one named last changes fastest.
Arguments:
- input_cells: bfloat16 [32, 64, 128, 128], P('depth', 'row'), may hold values from -6 to 6
- first_weight: bfloat16 [3, 3, 3, 64, 128], P(None, None, None, None, 'depth'), may hold values from -0.15625 to 0.15625
- second_weight: bfloat16 [3, 3, 3, 128, 256], P(None, None, None, None, 'depth'), may hold values from -0.109375 to 0.109375
Outputs:
- encoded: bfloat16 [8, 16, 32, 512], P('depth', 'row')
All inputs are finite; a program needn't handle non-finite values.
Results may differ from a plain program's by a relative error of at most 0.0049.
Values may be sent and summed in bfloat16 or wider, within the bound.
A program may use at most 64 MiB of HBM per device.

v0:
```python
import jax
import jax.numpy as jnp
from jax import lax
from jax.sharding import PartitionSpec as P


def from_behind(x, axis, by):
    count = lax.axis_size(axis)
    pairs = [(i, i + by) for i in range(count) if 0 <= i + by < count]
    return lax.ppermute(x, axis, pairs)


def stacked(weight, depth_tap, row_tap):
    kernel_taps = weight[depth_tap, row_tap]
    zeros_block = jnp.zeros_like(kernel_taps[0])
    upper_part = jnp.concatenate([kernel_taps[1], kernel_taps[2]], 0)
    lower_part = jnp.concatenate([zeros_block, kernel_taps[0]], 0)
    return jnp.concatenate([upper_part, lower_part], 1)


def convolve(extended, weight):
    planes = extended.shape[0] - 1
    row_count = extended.shape[1] - 1
    pair_count = extended.shape[2]
    features = extended.shape[3]
    out_width = weight.shape[4]
    running = jnp.zeros((planes // 2 * (row_count // 2) * pair_count, 2 * out_width), jnp.float32)
    for depth_tap in range(3):
        for row_tap in range(3):
            window = extended[depth_tap : depth_tap + planes : 2, row_tap : row_tap + row_count : 2]
            running = running + jnp.dot(
                window.reshape(-1, features),
                stacked(weight, depth_tap, row_tap),
                preferred_element_type=jnp.float32,
            )
    running = running.reshape(planes // 2, row_count // 2, pair_count, 2 * out_width)
    carried = jnp.pad(running[:, :, :-1, out_width:], ((0, 0), (0, 0), (1, 0), (0, 0)))
    return running[..., :out_width] + carried


def finish(field):
    activated = jnp.maximum(field, 0.0).astype(jnp.bfloat16)
    shape_now = activated.shape
    return activated.reshape(shape_now[0], shape_now[1], shape_now[2] // 2, 2 * shape_now[3])


def per_device(input_cells, first_weight, second_weight):
    first_full, second_full = (
        lax.all_gather(first_weight, "depth", axis=4, tiled=True),
        lax.all_gather(second_weight, "depth", axis=4, tiled=True),
    )
    below_plane = from_behind(input_cells[-1:], "depth", 1)
    with_plane = jnp.concatenate([below_plane, input_cells], 0)
    below_row = from_behind(with_plane[:, -1:], "row", 1)
    extended = jnp.concatenate([below_row, with_plane], 1)
    hidden = finish(convolve(extended, first_full))
    hidden_below = from_behind(hidden[-1:], "depth", 1)
    hidden_plus = jnp.concatenate([hidden_below, hidden], 0)
    hidden_rowrim = from_behind(hidden_plus[:, -1:], "row", 1)
    hidden_ext = jnp.concatenate([hidden_rowrim, hidden_plus], 1)
    summed = convolve(hidden_ext, second_full)
    return finish(summed)


def solution(mesh):
    return jax.shard_map(
        per_device,
        mesh=mesh,
        in_specs=(
            P("depth", "row", None, None),
            P(None, None, None, None, "depth"),
            P(None, None, None, None, "depth"),
        ),
        out_specs=P("depth", "row", None, None),
        check_vma=False,
    )
```

profile of v0, /device:TPU:22, one launch (start us, length us, event | category | flops | bytes accessed | tf_op | source)
XLA Modules:
  0.0 72.2 jit_solution(71455804238040424)
XLA Ops:
  6.5 0.0 all-gather.2.cloned.1.call-start
  6.5 0.7 all-gather.2.cloned.1.call-update
  7.3 1.1 %slice.378 = bf16[1,16,128,128]{3,2,1,0:T(8,128)(2,1)S(1)} slice(bf16[4,16,128,128]{3,2,1,0:T(8,128)(2,1)} %param.3), slice={[3:4], [0:16], [0:128], [0:128]} | slice | bytes 1048576 | tf_op jit(solution)/shard_map/slice | solution.py:52
  8.3 0.0 copy-start.2
  8.4 2.1 %collective-permute-start = (bf16[1,16,128,128]{3,2,1,0:T(8,128)(2,1)S(1)}, bf16[1,16,128,128]{3,2,1,0:T(8,128)(2,1)S(1)}, u32[]{:S(2)}, u32[]{:S(2)}) collective-permute-start(bf16[1,16,128,128]{3,2,1,0:T(8,128)(2,1)S(1)} %slice.378), channel_id=1, source_target_pairs={{0,4},{4,8},{8,12},{12,16},{16,20},{20,24},{24,28},{1,5},{5,9},{9,... | collective-permute-start | bytes 1572872 | tf_op jit(solution)/shard_map/ppermute | solution.py:10
  10.4 1.7 %fusion.230 = (bf16[2,8,128,128]{3,2,1,0:T(8,128)(2,1)S(1)}, bf16[2,8,128,128]{3,2,1,0:T(8,128)(2,1)S(1)}, bf16[2,8,128,128]{3,2,1,0:T(8,128)(2,1)S(1)}, bf16[2,8,128,128]{3,2,1,0:T(8,128)(2,1)S(1)}) fusion(bf16[4,16,128,128]{3,2,1,0:T(8,128)(2,1)} %param.3), kind=kLoop, calls=%fused_computation.291 | loop fusion | bytes 4194304 | tf_op jit(solution)/shard_map/slice | solution.py:30
  12.1 0.0 copy-done.2
  12.1 19.7 %all_gather.6 = bf16[3,3,3,64,128]{3,4,2,1,0:T(8,128)(2,1)S(1)} all-gather(bf16[3,3,3,64,16]{3,4,2,1,0:T(8,128)(2,1)S(1)} %copy-done.2), channel_id=1, replica_groups=mesh['depth'=8,'row'=4] {'depth'}, dimensions={4}, use_global_device_ids=true | all-gather | bytes 497664 | tf_op jit(solution)/shard_map/all_gather | solution.py:49
  31.9 0.5 convolution_bitcast_fusion.3
  32.4 0.0 copy-start
  32.4 0.5 convolution_bitcast_fusion.1
  33.0 0.0 collective-permute-done
  33.0 1.0 %copy-done = bf16[4,16,128,128]{3,2,1,0:T(8,128)(2,1)S(1)} copy-done((bf16[4,16,128,128]{3,2,1,0:T(8,128)(2,1)S(1)}, bf16[4,16,128,128]{3,2,1,0:T(8,128)(2,1)}, u32[]{:S(2)}) %copy-start) | copy-done | bytes 2097176
  34.0 0.3 constant_dynamic-update-slice_fusion
  34.3 0.1 fusion.229
  34.4 3.5 %collective-permute-start.1 = (bf16[5,1,128,128]{3,2,1,0:T(8,128)(2,1)S(1)}, bf16[5,1,128,128]{3,2,1,0:T(8,128)(2,1)S(1)}, u32[]{:S(2)}, u32[]{:S(2)}) collective-permute-start(bf16[5,1,128,128]{3,2,1,0:T(8,128)(2,1)S(1)} %slice.459), channel_id=1, source_target_pairs={{0,1},{1,2},{2,3},{4,5},{5,6},{6,7},{8,9},{9,10},{10,11},{12,13},{... | collective-permute-start | bytes 491528 | tf_op jit(solution)/shard_map/ppermute | solution.py:10
  37.9 0.5 fusion.106
  38.4 0.5 fusion.103
  38.9 3.8 %collective-permute-done.1 = bf16[5,1,128,128]{3,2,1,0:T(8,128)(2,1)S(1)} collective-permute-done((bf16[5,1,128,128]{3,2,1,0:T(8,128)(2,1)S(1)}, bf16[5,1,128,128]{3,2,1,0:T(8,128)(2,1)S(1)}, u32[]{:S(2)}, u32[]{:S(2)}) %collective-permute-start.1) | collective-permute-done | bytes 163872 | tf_op jit(solution)/shard_map/ppermute | solution.py:10
  42.7 0.2 pad_maximum_fusion
  43.0 0.2 fusion.228
  43.2 0.5 fusion.4
  43.7 0.5 fusion.3
  44.2 0.5 fusion
  44.8 0.6 fusion.2
  45.4 0.5 fusion.1
  45.9 0.1 slice.488
  46.0 0.2 fusion.6
  46.2 0.1 slice.419
  46.3 1.9 %collective-permute-start.2 = (bf16[1,8,64,256]{3,2,1,0:T(8,128)(2,1)S(1)}, bf16[1,8,64,256]{3,2,1,0:T(8,128)(2,1)S(1)}, u32[]{:S(2)}, u32[]{:S(2)}) collective-permute-start(bf16[1,8,64,256]{3,2,1,0:T(8,128)(2,1)S(1)} %slice.419), channel_id=1, source_target_pairs={{0,4},{4,8},{8,12},{12,16},{16,20},{20,24},{24,28},{1,5},{5,9},{9,... | collective-permute-start | bytes 786440 | tf_op jit(solution)/shard_map/ppermute | solution.py:10
  48.3 0.2 reshape.185
  48.5 5.5 %collective-permute-done.2 = bf16[1,8,64,256]{3,2,1,0:T(8,128)(2,1)S(1)} collective-permute-done((bf16[1,8,64,256]{3,2,1,0:T(8,128)(2,1)S(1)}, bf16[1,8,64,256]{3,2,1,0:T(8,128)(2,1)S(1)}, u32[]{:S(2)}, u32[]{:S(2)}) %collective-permute-start.2) | collective-permute-done | bytes 262176 | tf_op jit(solution)/shard_map/ppermute | solution.py:10
  54.1 3.5 %collective-permute-start.3 = (bf16[3,1,64,256]{3,2,1,0:T(8,128)(2,1)S(1)}, bf16[3,1,64,256]{3,2,1,0:T(8,128)(2,1)S(1)}, u32[]{:S(2)}, u32[]{:S(2)}) collective-permute-start(bf16[3,1,64,256]{3,2,1,0:T(8,128)(2,1)S(1)} %slice.490), channel_id=1, source_target_pairs={{0,1},{1,2},{2,3},{4,5},{5,6},{6,7},{8,9},{9,10},{10,11},{12,13},{... | collective-permute-start | bytes 294920 | tf_op jit(solution)/shard_map/ppermute | solution.py:10
  57.6 3.0 %collective-permute-done.3 = bf16[3,1,64,256]{3,2,1,0:T(8,128)(2,1)S(1)} collective-permute-done((bf16[3,1,64,256]{3,2,1,0:T(8,128)(2,1)S(1)}, bf16[3,1,64,256]{3,2,1,0:T(8,128)(2,1)S(1)}, u32[]{:S(2)}, u32[]{:S(2)}) %collective-permute-start.3) | collective-permute-done | bytes 98336 | tf_op jit(solution)/shard_map/ppermute | solution.py:10
  60.6 0.1 pad_maximum_fusion.1
  60.7 0.0 all-gather.2.cloned.1.call-done
  60.8 0.0 copy-start.1
  60.8 1.2 %slice_bitcast_fusion.20 = (bf16[128,256]{0,1:T(8,128)(2,1)S(1)}, bf16[128,256]{0,1:T(8,128)(2,1)S(1)}, bf16[128,256]{0,1:T(8,128)(2,1)S(1)}, bf16[128,256]{0,1:...) fusion(bf16[3,3,3,128,256]{3,4,2,1,0:T(8,128)(2,1)} %all-gather, ...), kind=kLoop, calls=%fused_computation.143 | loop fusion | bytes 1048576 | tf_op jit(solution)/shard_map/squeeze | solution.py:16
  62.0 0.3 fusion.19
  62.3 0.3 convolution_add_fusion.10
  62.5 0.0 copy-done.1
  62.6 0.1 slice_bitcast_fusion.2
  62.7 0.3 convolution_add_fusion.9
  62.9 0.3 convolution_add_fusion.8
  63.2 0.3 convolution_add_fusion.7
  63.5 0.3 convolution_add_fusion.6
  63.8 0.3 convolution_add_fusion.5
  64.0 0.3 convolution_add_fusion.4
  64.3 0.3 convolution_add_fusion.3
  64.6 0.1 fusion.36
  64.6 0.7 reshape.196
  (12 shorter events, 0.3 us)
Async XLA Ops:
  6.5 54.2 %all-gather.2.cloned.1.call-start = ((), (), s32[]{:S(2)}) async-start(), calls=%async_computation | async-start | bytes 1990656 | tf_op jit(solution)/shard_map/all_gather | solution.py:50
  8.3 3.8 %copy-start.2 = (bf16[3,3,3,64,16]{3,4,2,1,0:T(8,128)(2,1)S(1)}, bf16[3,3,3,64,16]{3,4,2,1,0:T(8,128)(2,1)}, u32[]{:S(2)}) copy-start(bf16[3,3,3,64,16]{3,4,2,1,0:T(8,128)(2,1)} %param.4) | copy-start | bytes 165892
  8.4 24.6 %collective-permute-start = (bf16[1,16,128,128]{3,2,1,0:T(8,128)(2,1)S(1)}, bf16[1,16,128,128]{3,2,1,0:T(8,128)(2,1)S(1)}, u32[]{:S(2)}, u32[]{:S(2)}) collective-permute-start(bf16[1,16,128,128]{3,2,1,0:T(8,128)(2,1)S(1)} %slice.378), channel_id=1, source_target_pairs={{0,4},{4,8},{8,12},{12,16},{16,20},{20,24},{24,28},{1,5},{5,9},{9,... | collective-permute-start | bytes 1572872 | tf_op jit(solution)/shard_map/ppermute | solution.py:10
  32.4 1.6 %copy-start = (bf16[4,16,128,128]{3,2,1,0:T(8,128)(2,1)S(1)}, bf16[4,16,128,128]{3,2,1,0:T(8,128)(2,1)}, u32[]{:S(2)}) copy-start(bf16[4,16,128,128]{3,2,1,0:T(8,128)(2,1)} %param.3) | copy-start | bytes 6291460
  34.4 8.3 %collective-permute-start.1 = (bf16[5,1,128,128]{3,2,1,0:T(8,128)(2,1)S(1)}, bf16[5,1,128,128]{3,2,1,0:T(8,128)(2,1)S(1)}, u32[]{:S(2)}, u32[]{:S(2)}) collective-permute-start(bf16[5,1,128,128]{3,2,1,0:T(8,128)(2,1)S(1)} %slice.459), channel_id=1, source_target_pairs={{0,1},{1,2},{2,3},{4,5},{5,6},{6,7},{8,9},{9,10},{10,11},{12,13},{... | collective-permute-start | bytes 491528 | tf_op jit(solution)/shard_map/ppermute | solution.py:10
  46.3 7.7 %collective-permute-start.2 = (bf16[1,8,64,256]{3,2,1,0:T(8,128)(2,1)S(1)}, bf16[1,8,64,256]{3,2,1,0:T(8,128)(2,1)S(1)}, u32[]{:S(2)}, u32[]{:S(2)}) collective-permute-start(bf16[1,8,64,256]{3,2,1,0:T(8,128)(2,1)S(1)} %slice.419), channel_id=1, source_target_pairs={{0,4},{4,8},{8,12},{12,16},{16,20},{20,24},{24,28},{1,5},{5,9},{9,... | collective-permute-start | bytes 786440 | tf_op jit(solution)/shard_map/ppermute | solution.py:10
  54.1 6.5 %collective-permute-start.3 = (bf16[3,1,64,256]{3,2,1,0:T(8,128)(2,1)S(1)}, bf16[3,1,64,256]{3,2,1,0:T(8,128)(2,1)S(1)}, u32[]{:S(2)}, u32[]{:S(2)}) collective-permute-start(bf16[3,1,64,256]{3,2,1,0:T(8,128)(2,1)S(1)} %slice.490), channel_id=1, source_target_pairs={{0,1},{1,2},{2,3},{4,5},{5,6},{6,7},{8,9},{9,10},{10,11},{12,13},{... | collective-permute-start | bytes 294920 | tf_op jit(solution)/shard_map/ppermute | solution.py:10
  60.8 1.8 %copy-start.1 = (bf16[3,3,3,128,256]{3,4,2,1,0:T(8,128)(2,1)S(1)}, bf16[3,3,3,128,256]{3,4,2,1,0:T(8,128)(2,1)}, u32[]{:S(2)}) copy-start(bf16[3,3,3,128,256]{3,4,2,1,0:T(8,128)(2,1)} %all-gather.2.cloned.1.call-done) | copy-start | bytes 5308420
Sparse Core Ops, SparseCore 0:
  9.2 28.6 all-gather.1
where the time goes:
time: 72.5 us; the launch traced here: 72.2 us
  blocking collectives  19.7 us (27%)
  between operations  13.8 us (19%)
  waiting for transfers between devices  13.1 us (18%)
  starting transfers between devices  10.9 us (15%)
  matrix products  7.11 us (10%)
  local copies, waits for them, and re-layouts  7.02 us (10%)
    all_gather x1, blocking collectives, per_device(): lax.all_gather(first_weight, 'depth', axis=4, tiled=True)  19.7 us
    ppermute x4, waiting for transfers between devices, from_behind(): return lax.ppermute(x, axis, pairs)  12.4 us
    ppermute x4, starting transfers between devices, from_behind(): return lax.ppermute(x, axis, pairs)  10.9 us
    dot_general x18, matrix products, convolve(): jnp.dot(window.reshape(-1, features), stacked(weight, depth_tap, row_tap)...  7.11 us
    slice x6, local copies, waits for them, and re-layouts, convolve(): extended[depth_tap:depth_tap + planes:2, row_tap:row_tap + row_count:2]  2.07 us
  transfers between devices with their start and end apart: 5, of which 3 were waited for; matrix products, arithmetic and copies ran while one was open for 13% of the time, Pallas kernels for 0%

commit v1 on v0

--- a/solution.py
+++ b/solution.py
@@ -46,7 +46,7 @@
 
 def per_device(input_cells, first_weight, second_weight):
     first_full, second_full = (
-        lax.all_gather(first_weight, "depth", axis=4, tiled=True),
+        jnp.concatenate(lax.all_gather(first_weight, "depth"), axis=4),
         lax.all_gather(second_weight, "depth", axis=4, tiled=True),
     )
     below_plane = from_behind(input_cells[-1:], "depth", 1)

time: 72.5 us -> 68.3 us (0.942)
  blocking collectives: 19.7 us -> 14.7 us
  local copies, waits for them, and re-layouts: 7.02 us -> 8.21 us
    all_gather x1, blocking collectives: 19.7 us -> 14.7 us  [per_device(): lax.all_gather(first_weight, 'depth')]
  transfers between devices with their start and end apart: 5 -> 5, of which waited for: 3 -> 3; matrix products, arithmetic and copies ran while one was open for 13% -> 15% of each run, Pallas kernels for 0% -> 0%
where the time goes in v1:
time: 68.3 us; the launch traced here: 67.7 us
  blocking collectives  14.7 us (22%)
  between operations  13.8 us (20%)
  waiting for transfers between devices  12.4 us (18%)
  starting transfers between devices  10.9 us (16%)
  local copies, waits for them, and re-layouts  8.21 us (12%)
  matrix products  7.07 us (10%)
    all_gather x1, blocking collectives, per_device(): lax.all_gather(first_weight, 'depth')  14.7 us
    ppermute x4, waiting for transfers between devices, from_behind(): return lax.ppermute(x, axis, pairs)  11.7 us
    ppermute x4, starting transfers between devices, from_behind(): return lax.ppermute(x, axis, pairs)  10.9 us
    dot_general x18, matrix products, convolve(): jnp.dot(window.reshape(-1, features), stacked(weight, depth_tap, row_tap)...  7.07 us
    slice x6, local copies, waits for them, and re-layouts, convolve(): extended[depth_tap:depth_tap + planes:2, row_tap:row_tap + row_count:2]  2.78 us
    squeeze x4, local copies, waits for them, and re-layouts, stacked(): upper_part = jnp.concatenate([kernel_taps[1], kernel_taps[2]], 0)  1.38 us
  transfers between devices with their start and end apart: 5, of which 3 were waited for; matrix products, arithmetic and copies ran while one was open for 15% of the time, Pallas kernels for 0%

profile of v1, /device:TPU:22, one launch (start us, length us, event | category | flops | bytes accessed | tf_op | source)
XLA Modules:
  0.0 67.7 jit_solution(13232055000347203651)
XLA Ops:
  6.5 0.0 all-gather.3.cloned.1.call-start
  6.5 0.7 %all-gather.3.cloned.1.call-update = ((bf16[3,3,3,128,32]{3,4,2,1,0:T(8,128)(2,1)}), bf16[3,3,3,128,256]{3,4,2,1,0:T(8,128)(2,1)}) async-update(((), (), s32[]{:S(2)}) %all-gather.3.cloned.1.call-start, bf16[3,3,3,128,32]{3,4,2,1,0:T(8,128)(2,1)} %param.5) | async-update | bytes 2211864
  7.3 1.1 %slice.378 = bf16[1,16,128,128]{3,2,1,0:T(8,128)(2,1)S(1)} slice(bf16[4,16,128,128]{3,2,1,0:T(8,128)(2,1)} %param.3), slice={[3:4], [0:16], [0:128], [0:128]} | slice | bytes 1048576 | tf_op jit(solution)/shard_map/slice | solution.py:52
  8.3 0.0 copy-start.5
  8.4 2.1 %collective-permute-start = (bf16[1,16,128,128]{3,2,1,0:T(8,128)(2,1)S(1)}, bf16[1,16,128,128]{3,2,1,0:T(8,128)(2,1)S(1)}, u32[]{:S(2)}, u32[]{:S(2)}) collective-permute-start(bf16[1,16,128,128]{3,2,1,0:T(8,128)(2,1)S(1)} %slice.378), channel_id=1, source_target_pairs={{0,4},{4,8},{8,12},{12,16},{16,20},{20,24},{24,28},{1,5},{5,9},{9,... | collective-permute-start | bytes 1572872 | tf_op jit(solution)/shard_map/ppermute | solution.py:10
  10.4 1.7 %fusion.230 = (bf16[2,8,128,128]{3,2,1,0:T(8,128)(2,1)S(1)}, bf16[2,8,128,128]{3,2,1,0:T(8,128)(2,1)S(1)}, bf16[2,8,128,128]{3,2,1,0:T(8,128)(2,1)S(1)}, bf16[2,8,128,128]{3,2,1,0:T(8,128)(2,1)S(1)}) fusion(bf16[4,16,128,128]{3,2,1,0:T(8,128)(2,1)} %param.3), kind=kLoop, calls=%fused_computation.291 | loop fusion | bytes 4194304 | tf_op jit(solution)/shard_map/slice | solution.py:30
  12.1 0.0 copy-done.5
  12.2 14.7 %all-gather = bf16[24,3,3,64,16]{3,4,2,1,0:T(8,128)(2,1)S(1)} all-gather(bf16[3,3,3,64,16]{3,4,2,1,0:T(8,128)(2,1)S(1)} %copy-done.5), channel_id=2, replica_groups=mesh['depth'=8,'row'=4] {'depth'}, dimensions={0}, use_global_device_ids=true | all-gather | bytes 497664 | tf_op jit(solution)/shard_map/all_gather | solution.py:49
  26.8 0.2 copy.13
  27.1 0.5 convolution_bitcast_fusion.3
  27.6 0.0 copy-start
  27.7 0.5 convolution_bitcast_fusion.1
  28.2 0.0 collective-permute-done
  28.3 1.0 %copy-done = bf16[4,16,128,128]{3,2,1,0:T(8,128)(2,1)S(1)} copy-done((bf16[4,16,128,128]{3,2,1,0:T(8,128)(2,1)S(1)}, bf16[4,16,128,128]{3,2,1,0:T(8,128)(2,1)}, u32[]{:S(2)}) %copy-start) | copy-done | bytes 2097176
  29.2 0.3 constant_dynamic-update-slice_fusion
  29.5 0.1 fusion.229
  29.6 3.5 %collective-permute-start.1 = (bf16[5,1,128,128]{3,2,1,0:T(8,128)(2,1)S(1)}, bf16[5,1,128,128]{3,2,1,0:T(8,128)(2,1)S(1)}, u32[]{:S(2)}, u32[]{:S(2)}) collective-permute-start(bf16[5,1,128,128]{3,2,1,0:T(8,128)(2,1)S(1)} %slice.459), channel_id=1, source_target_pairs={{0,1},{1,2},{2,3},{4,5},{5,6},{6,7},{8,9},{9,10},{10,11},{12,13},{... | collective-permute-start | bytes 491528 | tf_op jit(solution)/shard_map/ppermute | solution.py:10
  33.1 0.5 fusion.106
  33.6 0.5 fusion.103
  34.1 3.8 %collective-permute-done.1 = bf16[5,1,128,128]{3,2,1,0:T(8,128)(2,1)S(1)} collective-permute-done((bf16[5,1,128,128]{3,2,1,0:T(8,128)(2,1)S(1)}, bf16[5,1,128,128]{3,2,1,0:T(8,128)(2,1)S(1)}, u32[]{:S(2)}, u32[]{:S(2)}) %collective-permute-start.1) | collective-permute-done | bytes 163872 | tf_op jit(solution)/shard_map/ppermute | solution.py:10
  38.0 0.2 pad_maximum_fusion
  38.2 0.2 fusion.228
  38.4 0.5 fusion.4
  38.9 0.5 fusion.3
  39.5 0.5 fusion
  40.0 0.6 fusion.2
  40.6 0.5 fusion.1
  41.2 0.1 slice.488
  41.2 0.2 fusion.6
  41.5 0.1 slice.419
  41.6 1.9 %collective-permute-start.2 = (bf16[1,8,64,256]{3,2,1,0:T(8,128)(2,1)S(1)}, bf16[1,8,64,256]{3,2,1,0:T(8,128)(2,1)S(1)}, u32[]{:S(2)}, u32[]{:S(2)}) collective-permute-start(bf16[1,8,64,256]{3,2,1,0:T(8,128)(2,1)S(1)} %slice.419), channel_id=1, source_target_pairs={{0,4},{4,8},{8,12},{12,16},{16,20},{20,24},{24,28},{1,5},{5,9},{9,... | collective-permute-start | bytes 786440 | tf_op jit(solution)/shard_map/ppermute | solution.py:10
  43.5 0.2 reshape.193
  43.7 0.7 %fusion.233 = (bf16[1,4,64,256]{3,2,1,0:T(8,128)(2,1)S(1)}, bf16[1,4,64,256]{3,2,1,0:T(8,128)(2,1)}, bf16[1,4,64,256]{3,2,1,0:T(8,128)(2,1)}, bf16[1,4,64,256]{3,2,1,0:T(8,128)(2,1)}) fusion(bf16[2,8,64,256]{3,2,1,0:T(8,128)(2,1)S(1)} %reshape.193), kind=kLoop, calls=%fused_computation.294 | loop fusion | bytes 1048576 | tf_op jit(solution)/shard_map/slice | solution.py:30
  44.5 4.8 %collective-permute-done.2 = bf16[1,8,64,256]{3,2,1,0:T(8,128)(2,1)S(1)} collective-permute-done((bf16[1,8,64,256]{3,2,1,0:T(8,128)(2,1)S(1)}, bf16[1,8,64,256]{3,2,1,0:T(8,128)(2,1)S(1)}, u32[]{:S(2)}, u32[]{:S(2)}) %collective-permute-start.2) | collective-permute-done | bytes 262176 | tf_op jit(solution)/shard_map/ppermute | solution.py:10
  49.4 3.5 %collective-permute-start.3 = (bf16[3,1,64,256]{3,2,1,0:T(8,128)(2,1)S(1)}, bf16[3,1,64,256]{3,2,1,0:T(8,128)(2,1)S(1)}, u32[]{:S(2)}, u32[]{:S(2)}) collective-permute-start(bf16[3,1,64,256]{3,2,1,0:T(8,128)(2,1)S(1)} %slice.490), channel_id=1, source_target_pairs={{0,1},{1,2},{2,3},{4,5},{5,6},{6,7},{8,9},{9,10},{10,11},{12,13},{... | collective-permute-start | bytes 294920 | tf_op jit(solution)/shard_map/ppermute | solution.py:10
  52.9 3.0 %collective-permute-done.3 = bf16[3,1,64,256]{3,2,1,0:T(8,128)(2,1)S(1)} collective-permute-done((bf16[3,1,64,256]{3,2,1,0:T(8,128)(2,1)S(1)}, bf16[3,1,64,256]{3,2,1,0:T(8,128)(2,1)S(1)}, u32[]{:S(2)}, u32[]{:S(2)}) %collective-permute-start.3) | collective-permute-done | bytes 98336 | tf_op jit(solution)/shard_map/ppermute | solution.py:10
  55.9 0.1 pad_maximum_fusion.1
  56.0 0.0 all-gather.3.cloned.1.call-done
  56.0 0.0 copy-start.1
  56.0 1.2 %slice_bitcast_fusion.20 = (bf16[128,256]{0,1:T(8,128)(2,1)S(1)}, bf16[128,256]{0,1:T(8,128)(2,1)S(1)}, bf16[128,256]{0,1:T(8,128)(2,1)S(1)}, bf16[128,256]{0,1:...) fusion(bf16[3,3,3,128,256]{3,4,2,1,0:T(8,128)(2,1)} %all-gather, ...), kind=kLoop, calls=%fused_computation.143 | loop fusion | bytes 1048576 | tf_op jit(solution)/shard_map/squeeze | solution.py:16
  57.3 0.3 fusion.19
  57.5 0.3 convolution_add_fusion.10
  57.8 0.0 copy-done.1
  57.8 0.0 copy-start.4
  57.8 0.1 slice_bitcast_fusion.2
  57.9 0.0 copy-start.3
  57.9 0.3 convolution_add_fusion.9
  58.2 0.3 convolution_add_fusion.8
  58.5 0.0 copy-start.2
  58.5 0.2 copy-done.4
  58.7 0.3 convolution_add_fusion.7
  59.0 0.0 copy-done.3
  59.0 0.3 convolution_add_fusion.6
  59.3 0.3 convolution_add_fusion.5
  59.5 0.0 copy-done.2
  59.5 0.3 convolution_add_fusion.4
  59.8 0.3 convolution_add_fusion.3
  60.1 0.1 fusion.36
  60.2 0.7 %reshape.204 = bf16[1,4,32,512]{3,2,1,0:T(8,128)(2,1)} reshape(bf16[1,4,64,256]{3,2,1,0:T(8,128)(2,1)S(1)} %fusion.36) | data formatting | bytes 262144 | tf_op jit(solution)/shard_map/reshape | solution.py:44
  (11 shorter events, 0.3 us)
Async XLA Ops:
  6.5 49.5 %all-gather.3.cloned.1.call-start = ((), (), s32[]{:S(2)}) async-start(), calls=%async_computation | async-start | bytes 1990656 | tf_op jit(solution)/shard_map/all_gather | solution.py:50
  8.3 3.8 %copy-start.5 = (bf16[3,3,3,64,16]{3,4,2,1,0:T(8,128)(2,1)S(1)}, bf16[3,3,3,64,16]{3,4,2,1,0:T(8,128)(2,1)}, u32[]{:S(2)}) copy-start(bf16[3,3,3,64,16]{3,4,2,1,0:T(8,128)(2,1)} %param.4) | copy-start | bytes 165892
  8.4 19.8 %collective-permute-start = (bf16[1,16,128,128]{3,2,1,0:T(8,128)(2,1)S(1)}, bf16[1,16,128,128]{3,2,1,0:T(8,128)(2,1)S(1)}, u32[]{:S(2)}, u32[]{:S(2)}) collective-permute-start(bf16[1,16,128,128]{3,2,1,0:T(8,128)(2,1)S(1)} %slice.378), channel_id=1, source_target_pairs={{0,4},{4,8},{8,12},{12,16},{16,20},{20,24},{24,28},{1,5},{5,9},{9,... | collective-permute-start | bytes 1572872 | tf_op jit(solution)/shard_map/ppermute | solution.py:10
  27.6 1.6 %copy-start = (bf16[4,16,128,128]{3,2,1,0:T(8,128)(2,1)S(1)}, bf16[4,16,128,128]{3,2,1,0:T(8,128)(2,1)}, u32[]{:S(2)}) copy-start(bf16[4,16,128,128]{3,2,1,0:T(8,128)(2,1)} %param.3) | copy-start | bytes 6291460
  29.6 8.4 %collective-permute-start.1 = (bf16[5,1,128,128]{3,2,1,0:T(8,128)(2,1)S(1)}, bf16[5,1,128,128]{3,2,1,0:T(8,128)(2,1)S(1)}, u32[]{:S(2)}, u32[]{:S(2)}) collective-permute-start(bf16[5,1,128,128]{3,2,1,0:T(8,128)(2,1)S(1)} %slice.459), channel_id=1, source_target_pairs={{0,1},{1,2},{2,3},{4,5},{5,6},{6,7},{8,9},{9,10},{10,11},{12,13},{... | collective-permute-start | bytes 491528 | tf_op jit(solution)/shard_map/ppermute | solution.py:10
  41.6 7.7 %collective-permute-start.2 = (bf16[1,8,64,256]{3,2,1,0:T(8,128)(2,1)S(1)}, bf16[1,8,64,256]{3,2,1,0:T(8,128)(2,1)S(1)}, u32[]{:S(2)}, u32[]{:S(2)}) collective-permute-start(bf16[1,8,64,256]{3,2,1,0:T(8,128)(2,1)S(1)} %slice.419), channel_id=1, source_target_pairs={{0,4},{4,8},{8,12},{12,16},{16,20},{20,24},{24,28},{1,5},{5,9},{9,... | collective-permute-start | bytes 786440 | tf_op jit(solution)/shard_map/ppermute | solution.py:10
  49.4 6.5 %collective-permute-start.3 = (bf16[3,1,64,256]{3,2,1,0:T(8,128)(2,1)S(1)}, bf16[3,1,64,256]{3,2,1,0:T(8,128)(2,1)S(1)}, u32[]{:S(2)}, u32[]{:S(2)}) collective-permute-start(bf16[3,1,64,256]{3,2,1,0:T(8,128)(2,1)S(1)} %slice.490), channel_id=1, source_target_pairs={{0,1},{1,2},{2,3},{4,5},{5,6},{6,7},{8,9},{9,10},{10,11},{12,13},{... | collective-permute-start | bytes 294920 | tf_op jit(solution)/shard_map/ppermute | solution.py:10
  56.0 1.8 %copy-start.1 = (bf16[3,3,3,128,256]{3,4,2,1,0:T(8,128)(2,1)S(1)}, bf16[3,3,3,128,256]{3,4,2,1,0:T(8,128)(2,1)}, u32[]{:S(2)}) copy-start(bf16[3,3,3,128,256]{3,4,2,1,0:T(8,128)(2,1)} %all-gather.3.cloned.1.call-done) | copy-start | bytes 5308420
  57.8 0.9 %copy-start.4 = (bf16[1,4,64,256]{3,2,1,0:T(8,128)(2,1)S(1)}, bf16[1,4,64,256]{3,2,1,0:T(8,128)(2,1)}, u32[]{:S(2)}) copy-start(bf16[1,4,64,256]{3,2,1,0:T(8,128)(2,1)} %get-tuple-element.76) | copy-start | bytes 393220
  57.9 1.1 %copy-start.3 = (bf16[1,4,64,256]{3,2,1,0:T(8,128)(2,1)S(1)}, bf16[1,4,64,256]{3,2,1,0:T(8,128)(2,1)}, u32[]{:S(2)}) copy-start(bf16[1,4,64,256]{3,2,1,0:T(8,128)(2,1)} %get-tuple-element.75) | copy-start | bytes 393220
  58.5 1.1 %copy-start.2 = (bf16[1,4,64,256]{3,2,1,0:T(8,128)(2,1)S(1)}, bf16[1,4,64,256]{3,2,1,0:T(8,128)(2,1)}, u32[]{:S(2)}) copy-start(bf16[1,4,64,256]{3,2,1,0:T(8,128)(2,1)} %get-tuple-element.74) | copy-start | bytes 393220
Sparse Core Ops, SparseCore 0:
  9.2 28.3 all-gather.2
